TPU v7x, 32 devices: a whole 2x2x4 slice. The times are simulated.
32 devices in a mesh: seq: 8 (over y, x, core), ch: 4 (over z).
Axes of the slice: x: 2, y: 2, z: 4, core: 2. Of those that a mesh axis runs over, the one named last changes fastest.
Arguments:
- token_ids: int32 [2048], P('seq'), may hold values from 65 to 84, as said below
- embedding: bfloat16 [512, 8192], P(None, 'ch'), may hold values from -1200 to 1200
- norm_gain: float32 [8192], P('ch'), may hold values from 0.5 to 1.5
- conv_weight: float32 [3, 7, 8192], P(None, None, 'ch'), may hold values from -2 to 2
- pole_rates: float32 [16, 8192], P(None, 'ch'), may hold values from 0.001 to 0.105
- residues: float32 [16, 8192], P(None, 'ch'), may hold values from -70 to 70
- skip_gain: float32 [8192], P('ch'), may hold values from -1.5 to 1.5
- cotangent: bfloat16 [2048, 8192], P('seq', 'ch'), may hold values from -6 to 6
Outputs:
- hyena_out: bfloat16 [2048, 8192], P('seq', 'ch')
- grad_normed: bfloat16 [2048, 8192], P('seq', 'ch')
- grad_conv: float32 [3, 7, 8192], P(None, None, 'ch')
- grad_residues: float32 [16, 8192], P(None, 'ch')
- grad_skip: float32 [8192], P('ch')
Inputs may be any that keep to these rules, and one draw needn't show every extreme that they name: `token_ids`: every token is the byte code of A, C, G or T.
All inputs are finite; a program needn't handle non-finite values.
Results may differ from a plain program's by a relative error of at most 0.03.
Values may be sent and summed in bfloat16 or wider, within the bound.
A program may use at most 128 MiB of HBM per device.

v0:
```python
import functools

import jax
import jax.numpy as jnp
from jax import lax
from jax.experimental import pallas as pl
from jax.experimental.pallas import tpu as pltpu
from jax.sharding import PartitionSpec as P

TAPS = 7
CODES = (65, 67, 71, 84)
MESH = pl.DeviceIdType.MESH
F32 = jnp.float32
BF16 = jnp.bfloat16
LANES = 128
SUB = 8
UNROLL = 8
BAND = 32
VLIMIT = 60 * 1024 * 1024


def greet(peers):
    barrier = pltpu.get_barrier_semaphore()
    for peer in peers:
        pl.semaphore_signal(barrier, inc=1, device_id=peer, device_id_type=MESH)
    pl.semaphore_wait(barrier, len(peers))


def remote(src, dst, send_sem, recv_sem, peer):
    return pltpu.make_async_remote_copy(
        src_ref=src, dst_ref=dst, send_sem=send_sem, recv_sem=recv_sem,
        device_id=peer, device_id_type=MESH,
    )


def mega_kernel(
    n_seq, n_ch, poles,
    ids_ref, emb_ref, gain_ref, w_ref, rate_ref, res_ref, skip_in_ref, ct_ref,
    hyena_ref, gn_ref, conv_ref, gr_out_ref, gskip_out_ref,
    part, ss_got, prev_got, feat_ref, y_ref, gm_ref, ot_ref, n4_ref, ends_ref, in_ref, gr_ref, gskip_ref,
    p_ref, r_ref, decay_ref, skip_ref, xs, gs, table, got, out, fg_ref, head_ref, tail,
    terms, terms_ref, tgot, total, sums_ref, wide, pad,
    emb_rows, emb_sem, ss_send, ss_recv, halo_sem, f_send, f_recv, fb_send, fb_recv, a_send, a_recv, ab_send, ab_recv,
    t_send, t_recv, tb_send, tb_recv,
):
    me = lax.axis_index("seq")
    ch = lax.axis_index("ch")
    length, chans = ct_ref.shape
    width = chans * n_ch
    nb = chans // LANES
    lines = poles * nb
    first = lines + nb
    rows_used = first + 3 * TAPS * nb
    peer = [lax.rem(me + o, n_seq) for o in range(n_seq)]
    ch_peer = [lax.rem(ch + o, n_ch) for o in range(n_ch)]

    low_row = min(CODES) // BAND * BAND
    fetch = pltpu.make_async_copy(emb_ref.at[low_row : low_row + BAND, :], emb_rows, emb_sem)
    fetch.start()
    for k in range(nb):
        lanes = slice(k * LANES, (k + 1) * LANES)
        rates = rate_ref[:, lanes]
        rows = pl.ds(k, poles, stride=nb)
        p_ref[rows, :] = jnp.exp(-rates)
        decay_ref[rows, :] = jnp.exp(-rates * length)
        r_ref[rows, :] = res_ref[:, lanes]
        skip_ref[k : k + 1, :] = skip_in_ref[:, lanes]
    fetch.wait()
    emb = jnp.concatenate(
        [emb_rows[v - low_row : v - low_row + 1, :].astype(F32) for v in CODES]
        + [jnp.zeros((SUB - len(CODES), chans), F32)],
        0,
    )
    squares = jnp.broadcast_to(jnp.sum(emb * emb, axis=1, keepdims=True), (SUB, LANES))
    part[...] = squares
    greet([{"seq": peer[o]} for o in range(1, n_seq)] + [{"ch": ch_peer[o]} for o in range(1, n_ch)])
    ids_copy = remote(ids_ref, prev_got, halo_sem.at[0], halo_sem.at[1], {"seq": peer[1]})
    ids_copy.start()
    copies = []
    for o in range(1, n_ch):
        copy = remote(part, ss_got.at[o], ss_send.at[o], ss_recv.at[o], {"ch": ch_peer[o]})
        copy.start()
        copies.append(copy)
    for o in range(1, n_ch):
        copies[o - 1].wait()
        squares = squares + ss_got[o]
    ids_copy.wait()
    prev = jnp.where(me > 0, prev_got[...], -1)
    scale = lax.rsqrt(squares / width + 1e-05)[:, :1]
    n4 = (emb * scale * gain_ref[...]).astype(BF16).astype(F32)
    n4_ref[...] = n4
    zero_rows = jnp.zeros((SUB, chans), F32)
    for f in range(3):
        full = jnp.concatenate(
            [w_ref[f, i : i + 1, :] * n4 for i in range(TAPS)] + [zero_rows], 0
        )
        high = full.astype(BF16)
        rest = full - high.astype(F32)
        mid = rest.astype(BF16)
        low = (rest - mid.astype(F32)).astype(BF16)
        table[f, 0 : 8 * SUB, :] = high
        table[f, 8 * SUB : 16 * SUB, :] = mid
        table[f, 16 * SUB : 24 * SUB, :] = low
    row = lax.broadcasted_iota(jnp.int32, (SUB, length), 0)
    code = jnp.full((SUB, length), -2, jnp.int32)
    for a, value in enumerate(CODES):
        code = jnp.where(row == a, value, code)
    ext = jnp.concatenate([prev, ids_ref[...]], 1)
    hits = [
        jnp.where(ext[:, length - i : 2 * length - i] == code, 1.0, 0.0).astype(F32) for i in range(TAPS)
    ] + [jnp.zeros((SUB, length), F32)]
    onehot = jnp.concatenate(hits, 0)
    ot_ref[...] = onehot.astype(BF16)
    picks = jnp.transpose(jnp.concatenate([onehot] * 3, 0)).astype(BF16)

    def features(kb, carry):
        lanes = pl.ds(pl.multiple_of(kb * 256, 256), 256)
        parts = []
        for f in range(3):
            val = jnp.dot(picks, table[f, :, lanes], preferred_element_type=F32).astype(BF16)
            feat_ref[f, :, lanes] = val
            parts.append(val.astype(F32))
        x = parts[1] * parts[2]
        g = ct_ref[:, lanes].astype(F32) * parts[0]
        for s in range(2):
            xs[pl.ds(kb * 2 + s, length, stride=nb), :] = x[:, s * LANES : (s + 1) * LANES]
            gs[pl.ds(kb * 2 + s, length, stride=nb), :] = g[:, s * LANES : (s + 1) * LANES]
        return carry

    lax.fori_loop(0, chans // 256, features, 0)


    rp = lines // n_seq
    chunk = lambda k: pl.ds(pl.multiple_of(k * rp, rp), rp)

    def send_ends(side, send, recv):
        started = []
        for o in range(1, n_seq):
            copy = remote(
                ends_ref.at[side, chunk(peer[o]), :], got.at[side, me], send.at[o], recv.at[o], {"seq": peer[o]}
            )
            copy.start()
            started.append(copy)
        got[side, me] = ends_ref[side, chunk(me), :]
        return started

    def send_carries(side, started, send, recv):
        for copy in started:
            copy.wait()
        decay = decay_ref[chunk(me), :]
        state = jnp.zeros_like(decay)
        for e in reversed(range(n_seq)) if side else range(n_seq):
            out[side, e] = state
            state = decay * state + got[side, e]
        started = []
        for o in range(1, n_seq):
            copy = remote(
                out.at[side, peer[o]], in_ref.at[side, chunk(me), :], send.at[o], recv.at[o], {"seq": peer[o]}
            )
            copy.start()
            started.append(copy)
        in_ref[side, chunk(me), :] = out[side, me]
        return started

    group = poles // 2
    zero = jnp.zeros((SUB, LANES), F32)
    for h in range(nb // SUB):
        skip = skip_ref[h * SUB : (h + 1) * SUB, :]
        at = [pl.ds(n * nb + h * SUB, SUB) for n in range(poles)]
        for half in range(2):
            mine = at[half * group : (half + 1) * group]
            p = [p_ref[a, :] for a in mine]
            r = [r_ref[a, :] for a in mine]

            def forward(step, carry):
                s, acc, sk = carry
                s, acc = list(s), list(acc)
                for u in range(UNROLL):
                    rows = pl.ds(pl.multiple_of((step * UNROLL + u) * nb + h * SUB, SUB), SUB)
                    x, g = xs[rows, :], gs[rows, :]
                    terms = []
                    for n in range(group):
                        s[n] = p[n] * s[n] + x
                        acc[n] = acc[n] + g * s[n]
                        terms.append(r[n] * s[n])
                    while len(terms) > 1:
                        terms = [terms[i] + terms[i + 1] for i in range(0, len(terms), 2)]
                    if half == 0:
                        y_ref[rows, :] = terms[0] + skip * x
                        sk = sk + g * x
                    else:
                        y_ref[rows, :] = y_ref[rows, :] + terms[0]
                return tuple(s), tuple(acc), sk

            s, acc, sk = lax.fori_loop(
                0, length // UNROLL, forward, ((zero,) * group, (zero,) * group, zero)
            )
            for n in range(group):
                ends_ref[0, mine[n], :] = s[n]
                gr_ref[mine[n], :] = acc[n]
            if half == 0:
                gskip_ref[h * SUB : (h + 1) * SUB, :] = sk

    f_copies = send_ends(0, f_send, f_recv)
    for h in range(nb // SUB):
        if h == 1:
            f_copies = send_carries(0, f_copies, fb_send, fb_recv)
        skip = skip_ref[h * SUB : (h + 1) * SUB, :]
        at = [pl.ds(n * nb + h * SUB, SUB) for n in range(poles)]
        p = [p_ref[a, :] for a in at]
        r = [r_ref[a, :] for a in at]

        def backward(step, s):
            s = list(s)
            for u in range(UNROLL):
                t = length - 1 - (step * UNROLL + u)
                rows = pl.ds(pl.multiple_of(t * nb + h * SUB, SUB), SUB)
                g = gs[rows, :]
                terms = []
                for n in range(poles):
                    s[n] = p[n] * s[n] + g
                    terms.append(r[n] * s[n])
                while len(terms) > 1:
                    terms = [terms[i] + terms[i + 1] for i in range(0, len(terms), 2)]
                gm_ref[rows, :] = terms[0] + skip * g
            return tuple(s)

        s = lax.fori_loop(0, length // UNROLL, backward, (zero,) * poles)
        for n in range(poles):
            ends_ref[1, at[n], :] = s[n]
    a_copies = send_ends(1, a_send, a_recv)
    for copy in f_copies:
        copy.wait()

    def corrections(side, ref):
        for h in range(nb // SUB):
            at = [pl.ds(n * nb + h * SUB, SUB) for n in range(poles)]
            p = [p_ref[a, :] for a in at]

            def correct(step, u):
                u = list(u)
                for v in range(UNROLL):
                    t = step * UNROLL + v
                    t = length - 1 - t if side else t
                    rows = pl.ds(pl.multiple_of(t * nb + h * SUB, SUB), SUB)
                    parts = list(u)
                    while len(parts) > 1:
                        parts = [parts[i] + parts[i + 1] for i in range(0, len(parts), 2)]
                    ref[rows, :] = ref[rows, :] + parts[0]
                    u = [u[n] * p[n] for n in range(poles)]
                return tuple(u)

            lax.fori_loop(
                0, length // UNROLL, correct,
                tuple(r_ref[a, :] * (p_ref[a, :] * in_ref[side, a, :]) for a in at),
            )

    corrections(0, y_ref)
    a_copies = send_carries(1, a_copies, ab_send, ab_recv)
    terms[0:lines, :] = gr_ref[...] + in_ref[0] * p_ref[...] * ends_ref[1]
    terms[lines:first, :] = gskip_ref[...]
    if rows_used < terms.shape[0]:
        terms[rows_used:, :] = jnp.zeros((terms.shape[0] - rows_used, LANES), F32)
    hits_t = ot_ref[...]

    def emit(f, k, lanes, val, n4):
        val = val.astype(BF16)
        fg_ref[f, :, lanes] = val
        head_ref[f, :, lanes] = val[:SUB, :]
        sums = jnp.dot(hits_t, val, preferred_element_type=F32)
        taps = [jnp.sum(sums[i * SUB : (i + 1) * SUB, :] * n4, axis=0, keepdims=True) for i in range(TAPS)]
        terms[pl.ds(first + f * TAPS * nb + k, TAPS, stride=nb), :] = jnp.concatenate(taps, 0)

    def query_outputs(k, carry):
        lanes = pl.ds(pl.multiple_of(k * LANES, LANES), LANES)
        y = y_ref[pl.ds(k, length, stride=nb), :]
        hyena_ref[:, lanes] = (feat_ref[0, :, lanes].astype(F32) * y).astype(BF16)
        emit(0, k, lanes, ct_ref[:, lanes].astype(F32) * y, n4_ref[:, lanes])
        return carry

    lax.fori_loop(0, nb, query_outputs, 0)
    for copy in a_copies:
        copy.wait()
    corrections(1, gm_ref)

    def key_outputs(k, carry):
        lanes = pl.ds(pl.multiple_of(k * LANES, LANES), LANES)
        gm = gm_ref[pl.ds(k, length, stride=nb), :]
        n4 = n4_ref[:, lanes]
        emit(1, k, lanes, gm * feat_ref[2, :, lanes].astype(F32), n4)
        emit(2, k, lanes, gm * feat_ref[1, :, lanes].astype(F32), n4)
        return carry

    lax.fori_loop(0, nb, key_outputs, 0)
    terms_ref[...] = terms[...].astype(BF16)

    rt = terms_ref.shape[0] // n_seq
    part_at = lambda k: pl.ds(pl.multiple_of(k * rt, rt), rt)
    halo = remote(head_ref, tail, halo_sem.at[2], halo_sem.at[3], {"seq": peer[n_seq - 1]})
    halo.start()
    t_copies = []
    for o in range(1, n_seq):
        copy = remote(terms_ref.at[part_at(peer[o]), :], tgot.at[o], t_send.at[o], t_recv.at[o], {"seq": peer[o]})
        copy.start()
        t_copies.append(copy)
    keep = jnp.where(me < n_seq - 1, 1.0, 0.0).astype(F32)
    block = 64
    inner = length - block

    def filtered(k, begin, end, base):
        lanes = pl.ds(pl.multiple_of(k * LANES, LANES), LANES)
        w = [w_ref[f, i : i + 1, lanes] for f in range(3) for i in range(TAPS)]
        for b in range(begin, end, block):
            acc = jnp.zeros((block, LANES), F32)
            for f in range(3):
                for i in range(TAPS):
                    acc = acc + w[f * TAPS + i] * pad[f, b - base + i : b - base + i + block, :]
            gn_ref[b : b + block, lanes] = acc.astype(BF16)

    def inner_rows(k, carry):
        lanes = pl.ds(pl.multiple_of(k * LANES, LANES), LANES)
        for f in range(3):
            pad[f, 0:length, :] = fg_ref[f, :, lanes].astype(F32)
        filtered(k, 0, inner, 0)
        return carry

    def last_rows(k, carry):
        lanes = pl.ds(pl.multiple_of(k * LANES, LANES), LANES)
        for f in range(3):
            pad[f, 0:block, :] = fg_ref[f, inner:length, lanes].astype(F32)
            pad[f, block : block + SUB, :] = tail[f, :, lanes].astype(F32) * keep
        filtered(k, inner, length, inner)
        return carry

    lax.fori_loop(0, nb // 2, inner_rows, 0)
    summed = terms_ref[part_at(me), :].astype(F32)
    for o in range(1, n_seq):
        t_copies[o - 1].wait()
        summed = summed + tgot[o].astype(F32)
    total[...] = summed.astype(BF16)
    t_copies = []
    for o in range(1, n_seq):
        copy = remote(total, sums_ref.at[part_at(me), :], tb_send.at[o], tb_recv.at[o], {"seq": peer[o]})
        copy.start()
        t_copies.append(copy)
    sums_ref[part_at(me), :] = summed.astype(BF16)
    lax.fori_loop(nb // 2, nb, inner_rows, 0)
    halo.wait()
    lax.fori_loop(0, nb, last_rows, 0)
    for copy in t_copies:
        copy.wait()
    wide[...] = sums_ref[...].astype(F32)
    for k in range(nb):
        lanes = slice(k * LANES, (k + 1) * LANES)
        gr_out_ref[:, lanes] = wide[pl.ds(k, poles, stride=nb), :]
        gskip_out_ref[:, lanes] = wide[lines + k : lines + k + 1, :]
        for f in range(3):
            conv_ref[f, :, lanes] = wide[pl.ds(first + f * TAPS * nb + k, TAPS, stride=nb), :]


def solution(mesh):
    n_seq, n_ch = mesh.shape["seq"], mesh.shape["ch"]
    dma = pltpu.SemaphoreType.DMA
    vmem = pltpu.VMEM

    def per_device(token_ids, embedding, norm_gain, conv_weight, pole_rates, residues, skip_gain, cotangent):
        length, chans = cotangent.shape
        poles = pole_rates.shape[0]
        nb = chans // LANES
        lines = poles * nb
        rp = lines // n_seq
        rows = lines + nb + 3 * TAPS * nb
        each = -(-rows // (16 * n_seq)) * 16
        tile = vmem((length * nb, LANES), F32)
        line = vmem((lines, LANES), F32)
        scratch = [
            vmem((SUB, LANES), F32), vmem((n_ch, SUB, LANES), F32), vmem((1, length), jnp.int32),
            vmem((3, length, chans), BF16), tile, tile, vmem((8 * SUB, length), BF16), vmem((SUB, chans), F32),
            vmem((2, lines, LANES), F32), vmem((2, lines, LANES), F32), line, vmem((nb, LANES), F32),
            line, line, line, vmem((nb, LANES), F32), tile, tile, vmem((3, 24 * SUB, chans), BF16),
            vmem((2, n_seq, rp, LANES), F32), vmem((2, n_seq, rp, LANES), F32),
            vmem((3, length, chans), BF16), vmem((3, SUB, chans), BF16), vmem((3, SUB, chans), BF16),
            vmem((each * n_seq, LANES), F32), vmem((each * n_seq, LANES), BF16),
            vmem((n_seq, each, LANES), BF16), vmem((each, LANES), BF16), vmem((each * n_seq, LANES), BF16),
            vmem((each * n_seq, LANES), F32), vmem((3, length + SUB, LANES), F32),
            vmem((BAND, chans), BF16), dma, dma((n_ch,)), dma((n_ch,)), dma((4,)),
        ] + [dma((n_seq,))] * 12
        outs = [
            ((length, chans), BF16), ((length, chans), BF16), ((3, TAPS, chans), F32), ((poles, chans), F32),
            ((1, chans), F32),
        ]
        ins = (
            token_ids.reshape(1, length), embedding, norm_gain.reshape(1, chans), conv_weight, pole_rates, residues,
            skip_gain.reshape(1, chans), cotangent,
        )
        hyena, grad_normed, conv, gr, gskip = pl.pallas_call(
            functools.partial(mega_kernel, n_seq, n_ch, poles),
            out_shape=[jax.ShapeDtypeStruct(shape, dtype) for shape, dtype in outs],
            in_specs=[
                pl.BlockSpec(memory_space=pl.ANY if i == 1 else pltpu.VMEM) for i in range(len(ins))
            ],
            out_specs=[pl.BlockSpec(memory_space=pltpu.VMEM)] * len(outs),
            scratch_shapes=scratch,
            compiler_params=pltpu.CompilerParams(
                vmem_limit_bytes=VLIMIT, collective_id=0, has_side_effects=True
            ),
        )(*ins)
        return hyena, grad_normed, conv, gr, gskip.reshape(chans)

    in_specs = (
        P("seq"), P(None, "ch"), P("ch"), P(None, None, "ch"), P(None, "ch"), P(None, "ch"), P("ch"), P("seq", "ch"),
    )
    out_specs = (P("seq", "ch"), P("seq", "ch"), P(None, None, "ch"), P(None, "ch"), P("ch"))
    return jax.shard_map(per_device, mesh=mesh, in_specs=in_specs, out_specs=out_specs, check_vma=False)
```

profile of v0, /device:TPU:0, one launch (start us, length us, event | category | flops | bytes accessed | tf_op | source)
XLA Modules:
  0.0 60.2 jit_solution(13933056847897932682)
XLA Ops:
  0.6 54.2 %shard_map.119 = (bf16[256,2048]{1,0:T(8,128)(2,1)}, bf16[256,2048]{1,0:T(8,128)(2,1)}, f32[3,7,2048]{2,1,0:T(8,128)}, f32[16,2048]{1,0:T(8,128)}, f32[1,2048]{1,0:T(1,128)}) custom-call(s32[1,256]{1,0:T(1,128)} %bitcast.7, bf16[512,2048]{1,0:T(8,128)(2,1)} %emb_ref.1, f32[1,2048]{1,0:T(1,128)} %bitcast.4, f32[3,7,2048]{2,1,0:T(8,128)} %w_ref.1, ...), custom_call_target="tpu_custom_call" | custom-call | tf_op jit(solution)/shard_map/pallas_call | solution.py:396
  54.8 0.0 copy-start
  54.8 0.0 copy-start.1
  54.8 0.0 copy-start.2
  54.8 0.0 copy-start.3
  54.8 2.4 %copy.18 = bf16[256,2048]{1,0:T(8,128)(2,1)} copy(bf16[256,2048]{1,0:T(8,128)(2,1)} %get-tuple-element.20) | data formatting | bytes 2097152
  57.2 0.0 copy-done
  57.2 1.0 %copy.19 = bf16[256,2048]{1,0:T(8,128)(2,1)} copy(bf16[256,2048]{1,0:T(8,128)(2,1)S(1)} %copy-done) | data formatting | bytes 2097152
  58.2 0.0 copy-done.1
  58.2 0.7 %copy.20 = f32[3,7,2048]{2,1,0:T(8,128)} copy(f32[3,7,2048]{2,1,0:T(8,128)S(1)} %copy-done.1) | data formatting | bytes 344064
  58.9 0.0 copy-done.2
  58.9 0.7 %copy.21 = f32[16,2048]{1,0:T(8,128)} copy(f32[16,2048]{1,0:T(8,128)S(1)} %copy-done.2) | data formatting | bytes 262144
  59.6 0.0 copy-done.3
  59.6 0.6 copy.22
Async XLA Ops:
  54.8 2.4 %copy-start = (bf16[256,2048]{1,0:T(8,128)(2,1)S(1)}, bf16[256,2048]{1,0:T(8,128)(2,1)}, u32[]{:S(2)}) copy-start(bf16[256,2048]{1,0:T(8,128)(2,1)} %get-tuple-element.21) | copy-start | bytes 3145732
  54.8 3.4 %copy-start.1 = (f32[3,7,2048]{2,1,0:T(8,128)S(1)}, f32[3,7,2048]{2,1,0:T(8,128)}, u32[]{:S(2)}) copy-start(f32[3,7,2048]{2,1,0:T(8,128)} %get-tuple-element.22) | copy-start | bytes 516100
  54.8 4.1 %copy-start.2 = (f32[16,2048]{1,0:T(8,128)S(1)}, f32[16,2048]{1,0:T(8,128)}, u32[]{:S(2)}) copy-start(f32[16,2048]{1,0:T(8,128)} %get-tuple-element.23) | copy-start | bytes 393220
  54.8 4.7 %copy-start.3 = (f32[1,2048]{1,0:T(1,128)S(1)}, f32[1,2048]{1,0:T(1,128)}, u32[]{:S(2)}) copy-start(f32[1,2048]{1,0:T(1,128)} %get-tuple-element.14) | copy-start | bytes 24580
where the time goes:
time: 60.3 us; the launch traced here: 60.2 us
  Pallas kernels  54.2 us (90%)
  local copies, waits for them, and re-layouts  5.32 us (9%)
  between operations  0.68 us (1%)
    pallas_call x1, Pallas kernels, per_device(): pl.pallas_call(functools.partial(mega_kernel, n_seq, n_ch, poles), out_sh...  54.2 us
    unnamed x13, local copies, waits for them, and re-layouts  5.32 us

commit v1 on v0

--- a/solution.py
+++ b/solution.py
@@ -23,7 +23,10 @@
     barrier = pltpu.get_barrier_semaphore()
     for peer in peers:
         pl.semaphore_signal(barrier, inc=1, device_id=peer, device_id_type=MESH)
-    pl.semaphore_wait(barrier, len(peers))
+
+
+def greeted(peers):
+    pl.semaphore_wait(pltpu.get_barrier_semaphore(), len(peers))
 
 
 def remote(src, dst, send_sem, recv_sem, peer):
@@ -35,8 +38,9 @@
 
 def mega_kernel(
     n_seq, n_ch, poles,
-    ids_ref, emb_ref, gain_ref, w_ref, rate_ref, res_ref, skip_in_ref, ct_ref,
+    ids_in, emb_ref, gain_in, w_in, rate_in, res_in, skip_in, ct_in,
     hyena_ref, gn_ref, conv_ref, gr_out_ref, gskip_out_ref,
+    ids_ref, gain_ref, w_ref, rate_ref, res_ref, skip_in_ref, ct_ref, load_sem,
     part, ss_got, prev_got, feat_ref, y_ref, gm_ref, ot_ref, n4_ref, ends_ref, in_ref, gr_ref, gskip_ref,
     p_ref, r_ref, decay_ref, skip_ref, xs, gs, table, got, out, fg_ref, head_ref, tail,
     terms, terms_ref, tgot, total, sums_ref, wide, pad,
@@ -54,9 +58,22 @@
     peer = [lax.rem(me + o, n_seq) for o in range(n_seq)]
     ch_peer = [lax.rem(ch + o, n_ch) for o in range(n_ch)]
 
+    peers = [{"seq": peer[o]} for o in range(1, n_seq)] + [{"ch": ch_peer[o]} for o in range(1, n_ch)]
+    greet(peers)
     low_row = min(CODES) // BAND * BAND
     fetch = pltpu.make_async_copy(emb_ref.at[low_row : low_row + BAND, :], emb_rows, emb_sem)
     fetch.start()
+    loads = [
+        pltpu.make_async_copy(src, dst, load_sem.at[i])
+        for i, (src, dst) in enumerate((
+            (rate_in, rate_ref), (res_in, res_ref), (skip_in, skip_in_ref), (ids_in, ids_ref), (gain_in, gain_ref),
+            (w_in, w_ref), (ct_in, ct_ref),
+        ))
+    ]
+    for load in loads:
+        load.start()
+    for load in loads[:3]:
+        load.wait()
     for k in range(nb):
         lanes = slice(k * LANES, (k + 1) * LANES)
         rates = rate_ref[:, lanes]
@@ -73,14 +90,16 @@
     )
     squares = jnp.broadcast_to(jnp.sum(emb * emb, axis=1, keepdims=True), (SUB, LANES))
     part[...] = squares
-    greet([{"seq": peer[o]} for o in range(1, n_seq)] + [{"ch": ch_peer[o]} for o in range(1, n_ch)])
-    ids_copy = remote(ids_ref, prev_got, halo_sem.at[0], halo_sem.at[1], {"seq": peer[1]})
+    greeted(peers)
+    ids_copy = remote(ids_in, prev_got, halo_sem.at[0], halo_sem.at[1], {"seq": peer[1]})
     ids_copy.start()
     copies = []
     for o in range(1, n_ch):
         copy = remote(part, ss_got.at[o], ss_send.at[o], ss_recv.at[o], {"ch": ch_peer[o]})
         copy.start()
         copies.append(copy)
+    for load in loads[3:6]:
+        load.wait()
     for o in range(1, n_ch):
         copies[o - 1].wait()
         squares = squares + ss_got[o]
@@ -127,6 +146,7 @@
             gs[pl.ds(kb * 2 + s, length, stride=nb), :] = g[:, s * LANES : (s + 1) * LANES]
         return carry
 
+    loads[6].wait()
     lax.fori_loop(0, chans // 256, features, 0)
 
 
@@ -358,6 +378,17 @@
             conv_ref[f, :, lanes] = wide[pl.ds(first + f * TAPS * nb + k, TAPS, stride=nb), :]
 
 
+def finish_kernel(hyena_in, gn_in, conv_in, gr_in, gskip_in, hyena_ref, gn_ref, conv_ref, gr_ref, gskip_ref, sem):
+    pairs = (
+        (hyena_in, hyena_ref), (gn_in, gn_ref), (conv_in, conv_ref), (gr_in, gr_ref), (gskip_in, gskip_ref),
+    )
+    copies = [pltpu.make_async_copy(src, dst, sem.at[i]) for i, (src, dst) in enumerate(pairs)]
+    for copy in copies:
+        copy.start()
+    for copy in copies:
+        copy.wait()
+
+
 def solution(mesh):
     n_seq, n_ch = mesh.shape["seq"], mesh.shape["ch"]
     dma = pltpu.SemaphoreType.DMA
@@ -374,6 +405,9 @@
         tile = vmem((length * nb, LANES), F32)
         line = vmem((lines, LANES), F32)
         scratch = [
+            vmem((1, length), jnp.int32), vmem((1, chans), F32), vmem((3, TAPS, chans), F32),
+            vmem((poles, chans), F32), vmem((poles, chans), F32), vmem((1, chans), F32), vmem((length, chans), BF16),
+            dma((7,)),
             vmem((SUB, LANES), F32), vmem((n_ch, SUB, LANES), F32), vmem((1, length), jnp.int32),
             vmem((3, length, chans), BF16), tile, tile, vmem((8 * SUB, length), BF16), vmem((SUB, chans), F32),
             vmem((2, lines, LANES), F32), vmem((2, lines, LANES), F32), line, vmem((nb, LANES), F32),
@@ -393,11 +427,11 @@
             token_ids.reshape(1, length), embedding, norm_gain.reshape(1, chans), conv_weight, pole_rates, residues,
             skip_gain.reshape(1, chans), cotangent,
         )
-        hyena, grad_normed, conv, gr, gskip = pl.pallas_call(
+        held = pl.pallas_call(
             functools.partial(mega_kernel, n_seq, n_ch, poles),
-            out_shape=[jax.ShapeDtypeStruct(shape, dtype) for shape, dtype in outs],
+            out_shape=[pltpu.VMEM(shape, dtype) for shape, dtype in outs],
             in_specs=[
-                pl.BlockSpec(memory_space=pl.ANY if i == 1 else pltpu.VMEM) for i in range(len(ins))
+                pl.BlockSpec(memory_space=pl.ANY) for i in range(len(ins))
             ],
             out_specs=[pl.BlockSpec(memory_space=pltpu.VMEM)] * len(outs),
             scratch_shapes=scratch,
@@ -405,6 +439,13 @@
                 vmem_limit_bytes=VLIMIT, collective_id=0, has_side_effects=True
             ),
         )(*ins)
+        hyena, grad_normed, conv, gr, gskip = pl.pallas_call(
+            finish_kernel,
+            out_shape=[jax.ShapeDtypeStruct(shape, dtype) for shape, dtype in outs],
+            in_specs=[pl.BlockSpec(memory_space=pltpu.VMEM)] * len(outs),
+            out_specs=[pl.BlockSpec(memory_space=pl.ANY)] * len(outs),
+            scratch_shapes=[dma((len(outs),))],
+        )(*(pltpu.with_memory_space_constraint(part, pltpu.VMEM) for part in held))
         return hyena, grad_normed, conv, gr, gskip.reshape(chans)
 
     in_specs = (

time: 60.3 us -> 52.6 us (0.87)
  local copies, waits for them, and re-layouts: 5.32 us -> 0 us
  Pallas kernels: 54.2 us -> 51.8 us
    unnamed x13 -> x0, local copies, waits for them, and re-layouts: 5.32 us -> none
    pallas_call x1, Pallas kernels: 54.2 us -> 50.3 us  [per_device(): pl.pallas_call(functools.partial(mega_kernel, n_seq, n_ch, poles), out_sh...]
    pallas_call x0 -> x1, Pallas kernels: none -> 1.46 us  [per_device(): pl.pallas_call(finish_kernel, out_shape=[jax.ShapeDtypeStruct(shape, dtyp...]
where the time goes in v1:
time: 52.6 us; the launch traced here: 52.4 us
  Pallas kernels  51.8 us (98%)
  between operations  0.64 us (1%)
    pallas_call x1, Pallas kernels, per_device(): pl.pallas_call(functools.partial(mega_kernel, n_seq, n_ch, poles), out_sh...  50.3 us
    pallas_call x1, Pallas kernels, per_device(): pl.pallas_call(finish_kernel, out_shape=[jax.ShapeDtypeStruct(shape, dtyp...  1.46 us

profile of v1, /device:TPU:0, one launch (start us, length us, event | category | flops | bytes accessed | tf_op | source)
XLA Modules:
  0.0 52.4 jit_solution(1897917024550465976)
XLA Ops:
  0.6 50.3 %shard_map.119 = (bf16[256,2048]{1,0:T(8,128)(2,1)S(1)}, bf16[256,2048]{1,0:T(8,128)(2,1)S(1)}, f32[3,7,2048]{2,1,0:T(8,128)S(1)}, f32[16,2048]{1,0:T(8,128)S(1)}, f32[1,2048]{1,0:T(1,128)S(1)}) custom-call(s32[1,256]{1,0:T(1,128)} %bitcast.6, bf16[512,2048]{1,0:T(8,128)(2,1)} %emb_ref.1, f32[1,2048]{1,0:T(1,128)} %bitcast.4, f32[3,7,2048]{2,1,0:T(8,128)} %w_in.1, ...), custom_call_target="tpu_custom_call" | custom-call | tf_op jit(solution)/shard_map/pallas_call | solution.py:430
  51.0 1.5 %shard_map.120 = (bf16[256,2048]{1,0:T(8,128)(2,1)}, bf16[256,2048]{1,0:T(8,128)(2,1)}, f32[3,7,2048]{2,1,0:T(8,128)}, f32[16,2048]{1,0:T(8,128)}, f32[1,2048]{1,0:T(1,128)}) custom-call(bf16[256,2048]{1,0:T(8,128)(2,1)S(1)} %get-tuple-element.15.hyena_in, bf16[256,2048]{1,0:T(8,128)(2,1)S(1)} %get-tuple-element.16.gn_in, ...), custom_call_target="tpu_custom_call" | custom-call | tf_op jit(solution)/shard_map/pallas_call | solution.py:442

commit v2 on v1

v2 whole, which is shorter than its diff:
```python
import functools

import jax
import jax.numpy as jnp
from jax import lax
from jax.experimental import pallas as pl
from jax.experimental.pallas import tpu as pltpu
from jax.sharding import PartitionSpec as P

TAPS = 7
CODES = (65, 67, 71, 84)
MESH = pl.DeviceIdType.MESH
F32 = jnp.float32
BF16 = jnp.bfloat16
LANES = 128
SUB = 8
CHUNK = 8
GAP = 8
PAIR = 2
BAND = 32
VLIMIT = 60 * 1024 * 1024


def greet(peers):
    barrier = pltpu.get_barrier_semaphore()
    for peer in peers:
        pl.semaphore_signal(barrier, inc=1, device_id=peer, device_id_type=MESH)


def greeted(peers):
    pl.semaphore_wait(pltpu.get_barrier_semaphore(), len(peers))


def remote(src, dst, send_sem, recv_sem, peer):
    return pltpu.make_async_remote_copy(
        src_ref=src, dst_ref=dst, send_sem=send_sem, recv_sem=recv_sem,
        device_id=peer, device_id_type=MESH,
    )


def mega_kernel(
    n_seq, n_ch, poles,
    ids_in, emb_ref, gain_in, w_in, rate_in, res_in, skip_in, ct_in,
    hyena_ref, gn_ref, conv_ref, gr_out_ref, gskip_out_ref,
    ids_ref, gain_ref, w_ref, rate_ref, res_ref, skip_in_ref, ct_ref, load_sem,
    part, ss_got, prev_got, feat_ref, y_ref, gm_ref, ot_ref, n4_ref, ends_ref, in_ref, gr_ref, gskip_ref,
    p_ref, rp_ref, pc_ref, hs_ref, lag_ref, s0_ref, b0_ref, decay_ref, xs, gs, table, got, out, fg_ref, head_ref, tail,
    terms_e, whole_e, tgot_e, total_e, sums_e, wide_e, terms_l, whole_l, tgot_l, total_l, sums_l, wide_l, pad,
    emb_rows, emb_sem, ss_send, ss_recv, halo_sem, f_send, f_recv, fb_send, fb_recv, a_send, a_recv, ab_send, ab_recv,
    t_send, t_recv, tb_send, tb_recv, l_send, l_recv, lb_send, lb_recv,
):
    me = lax.axis_index("seq")
    ch = lax.axis_index("ch")
    length, chans = ct_ref.shape
    width = chans * n_ch
    nb = chans // LANES
    pitch = nb + GAP
    lines = poles * nb
    first = lines + nb
    peer = [lax.rem(me + o, n_seq) for o in range(n_seq)]
    ch_peer = [lax.rem(ch + o, n_ch) for o in range(n_ch)]

    peers = [{"seq": peer[o]} for o in range(1, n_seq)] + [{"ch": ch_peer[o]} for o in range(1, n_ch)]
    greet(peers)
    low_row = min(CODES) // BAND * BAND
    fetch = pltpu.make_async_copy(emb_ref.at[low_row : low_row + BAND, :], emb_rows, emb_sem)
    fetch.start()
    loads = [
        pltpu.make_async_copy(src, dst, load_sem.at[i])
        for i, (src, dst) in enumerate((
            (rate_in, rate_ref), (res_in, res_ref), (skip_in, skip_in_ref), (ids_in, ids_ref), (gain_in, gain_ref),
            (w_in, w_ref), (ct_in, ct_ref),
        ))
    ]
    for load in loads:
        load.start()
    for load in loads[:3]:
        load.wait()
    for k in range(nb):
        lanes = slice(k * LANES, (k + 1) * LANES)
        rates = rate_ref[:, lanes]
        rows = pl.ds(k, poles, stride=nb)
        p_ref[rows, :] = jnp.exp(-rates)
        decay_ref[rows, :] = jnp.exp(-rates * length)
        pc_ref[rows, :] = jnp.exp(-rates * CHUNK)
        rp_ref[rows, :] = res_ref[:, lanes] * jnp.exp(-rates)
        weight = res_ref[:, lanes]
        for d in range(CHUNK):
            tap = jnp.sum(weight, axis=0, keepdims=True)
            hs_ref[d * nb + k : d * nb + k + 1, :] = tap + skip_in_ref[:, lanes] if d == 0 else tap
            weight = weight * jnp.exp(-rates)
    fetch.wait()
    emb = jnp.concatenate(
        [emb_rows[v - low_row : v - low_row + 1, :].astype(F32) for v in CODES]
        + [jnp.zeros((SUB - len(CODES), chans), F32)],
        0,
    )
    squares = jnp.broadcast_to(jnp.sum(emb * emb, axis=1, keepdims=True), (SUB, LANES))
    part[...] = squares
    greeted(peers)
    ids_copy = remote(ids_in, prev_got, halo_sem.at[0], halo_sem.at[1], {"seq": peer[1]})
    ids_copy.start()
    copies = []
    for o in range(1, n_ch):
        copy = remote(part, ss_got.at[o], ss_send.at[o], ss_recv.at[o], {"ch": ch_peer[o]})
        copy.start()
        copies.append(copy)
    for load in loads[3:6]:
        load.wait()
    ids_copy.wait()
    prev = jnp.where(me > 0, prev_got[...], -1)
    row = lax.broadcasted_iota(jnp.int32, (SUB, length), 0)
    code = jnp.full((SUB, length), -2, jnp.int32)
    for a, value in enumerate(CODES):
        code = jnp.where(row == a, value, code)
    ext = jnp.concatenate([prev, ids_ref[...]], 1)
    hits = [
        jnp.where(ext[:, length - i : 2 * length - i] == code, 1.0, 0.0).astype(F32) for i in range(TAPS)
    ] + [jnp.zeros((SUB, length), F32)]
    onehot = jnp.concatenate(hits, 0)
    ot_ref[...] = onehot.astype(BF16)
    picks = jnp.transpose(jnp.concatenate([onehot] * 2, 0)).astype(BF16)
    for o in range(1, n_ch):
        copies[o - 1].wait()
        squares = squares + ss_got[o]
    scale = lax.rsqrt(squares / width + 1e-05)[:, :1]
    n4 = (emb * scale * gain_ref[...]).astype(BF16).astype(F32)
    n4_ref[...] = n4
    zero_rows = jnp.zeros((SUB, chans), F32)
    for f in range(3):
        full = jnp.concatenate(
            [w_ref[f, i : i + 1, :] * n4 for i in range(TAPS)] + [zero_rows], 0
        )
        high = full.astype(BF16)
        rest = full - high.astype(F32)
        table[f, 0 : 8 * SUB, :] = high
        table[f, 8 * SUB : 16 * SUB, :] = rest.astype(BF16)

    def features(kb, carry):
        lanes = pl.ds(pl.multiple_of(kb * 256, 256), 256)
        parts = []
        for f in range(3):
            val = jnp.dot(picks, table[f, :, lanes], preferred_element_type=F32).astype(BF16)
            feat_ref[f, :, lanes] = val
            parts.append(val.astype(F32))
        x = parts[1] * parts[2]
        g = ct_ref[:, lanes].astype(F32) * parts[0]
        for s in range(2):
            xs[pl.ds(kb * 2 + s, length, stride=pitch), :] = x[:, s * LANES : (s + 1) * LANES]
            gs[pl.ds(kb * 2 + s, length, stride=pitch), :] = g[:, s * LANES : (s + 1) * LANES]
        return carry

    loads[6].wait()
    lax.fori_loop(0, chans // 256, features, 0)


    rp = lines // n_seq
    chunk = lambda k: pl.ds(pl.multiple_of(k * rp, rp), rp)

    def send_ends(side, send, recv):
        started = []
        for o in range(1, n_seq):
            copy = remote(
                ends_ref.at[side, chunk(peer[o]), :], got.at[side, me], send.at[o], recv.at[o], {"seq": peer[o]}
            )
            copy.start()
            started.append(copy)
        got[side, me] = ends_ref[side, chunk(me), :]
        return started

    def send_carries(side, started, send, recv):
        for copy in started:
            copy.wait()
        decay = decay_ref[chunk(me), :]
        state = jnp.zeros_like(decay)
        for e in reversed(range(n_seq)) if side else range(n_seq):
            out[side, e] = state
            state = decay * state + got[side, e]
        started = []
        for o in range(1, n_seq):
            copy = remote(
                out.at[side, peer[o]], in_ref.at[side, chunk(me), :], send.at[o], recv.at[o], {"seq": peer[o]}
            )
            copy.start()
            started.append(copy)
        in_ref[side, chunk(me), :] = out[side, me]
        return started

    group = poles // 2
    zero = jnp.zeros((SUB, LANES), F32)
    halves = range(nb // SUB)
    chunks = length // CHUNK
    at = [[pl.ds(n * nb + h * SUB, SUB) for n in range(poles)] for h in halves]

    def row(ref_row, h):
        return pl.ds(pl.multiple_of(ref_row * nb + h * SUB, SUB), SUB)

    def time(t, h):
        return pl.ds(pl.multiple_of(t * pitch + h * SUB, SUB), SUB)

    def tree(values):
        values = list(values)
        while len(values) > 1:
            values = [
                values[i] + values[i + 1] if i + 1 < len(values) else values[i] for i in range(0, len(values), 2)
            ]
        return values[0]

    for h in halves:
        for half in range(2):
            poles_of = range(half * group, (half + 1) * group)
            p = [p_ref[at[h][n], :] for n in poles_of]
            pc = [pc_ref[at[h][n], :] for n in poles_of]

            def states(step, s):
                s = list(s)
                for c in range(PAIR):
                    u = step * PAIR + c
                    for i, n in enumerate(poles_of):
                        s0_ref[row(u * poles + n, h), :] = s[i]
                    for v in range(CHUNK):
                        x = xs[time(u * CHUNK + v, h), :]
                        e = [p[i] * e[i] + x for i in range(group)] if v else [x] * group
                    s = [pc[i] * s[i] + e[i] for i in range(group)]
                return tuple(s)

            s = lax.fori_loop(0, chunks // PAIR, states, (zero,) * group)
            for i, n in enumerate(poles_of):
                ends_ref[0, at[h][n], :] = s[i]

    f_copies = send_ends(0, f_send, f_recv)
    for h in halves:
        for half in range(2):
            poles_of = range(half * group, (half + 1) * group)
            p = [p_ref[at[h][n], :] for n in poles_of]
            pc = [pc_ref[at[h][n], :] for n in poles_of]

            def adjoints(step, carry):
                s, acc = list(carry[0]), list(carry[1])
                for c in range(PAIR):
                    u = chunks - 1 - (step * PAIR + c)
                    for i, n in enumerate(poles_of):
                        b0_ref[row(u * poles + n, h), :] = s[i]
                    for v in reversed(range(CHUNK)):
                        g = gs[time(u * CHUNK + v, h), :]
                        e = [p[i] * e[i] + g for i in range(group)] if v < CHUNK - 1 else [g] * group
                    s = [pc[i] * s[i] + e[i] for i in range(group)]
                    acc = [acc[i] + s0_ref[row(u * poles + n, h), :] * e[i] for i, n in enumerate(poles_of)]
                return tuple(s), tuple(acc)

            s, acc = lax.fori_loop(0, chunks // PAIR, adjoints, ((zero,) * group, (zero,) * group))
            for i, n in enumerate(poles_of):
                ends_ref[1, at[h][n], :] = s[i]
                gr_ref[at[h][n], :] = acc[i]
    f_copies = send_carries(0, f_copies, fb_send, fb_recv)
    a_copies = send_ends(1, a_send, a_recv)

    for h in halves:
        taps = [hs_ref[row(d, h), :] for d in range(CHUNK)]

        def near(u, lag):
            lag = list(lag)
            x = [xs[time(u * CHUNK + v, h), :] for v in range(CHUNK)]
            g = [gs[time(u * CHUNK + v, h), :] for v in range(CHUNK)]
            for v in range(CHUNK):
                y_ref[time(u * CHUNK + v, h), :] = tree(taps[d] * x[v - d] for d in range(v + 1))
                gm_ref[time(u * CHUNK + v, h), :] = tree(taps[d] * g[v + d] for d in range(CHUNK - v))
            for d in range(CHUNK):
                lag[d] = lag[d] + tree(g[v + d] * x[v] for v in range(CHUNK - d))
            return tuple(lag)

        lag = lax.fori_loop(0, chunks, near, (zero,) * CHUNK)
        gskip_ref[h * SUB : (h + 1) * SUB, :] = lag[0]
        for n in range(poles):
            p = p_ref[at[h][n], :]
            total_lag = lag[CHUNK - 1]
            for d in reversed(range(CHUNK - 1)):
                total_lag = p * total_lag + lag[d]
            lag_ref[at[h][n], :] = total_lag
    for copy in f_copies:
        copy.wait()
    a_copies = send_carries(1, a_copies, ab_send, ab_recv)

    def far(side, kept, ref):
        for h in halves:
            p = [p_ref[at[h][n], :] for n in range(poles)]

            def readout(step, w):
                u = chunks - 1 - step if side else step
                part = [rp_ref[at[h][n], :] * kept[row(u * poles + n, h), :] + w[n] for n in range(poles)]
                for v in reversed(range(CHUNK)) if side else range(CHUNK):
                    rows = time(u * CHUNK + v, h)
                    ref[rows, :] = ref[rows, :] + tree(part)
                    part = [part[n] * p[n] for n in range(poles)]
                return tuple(w[n] * pc_ref[at[h][n], :] for n in range(poles))

            lax.fori_loop(0, chunks, readout, tuple(rp_ref[a, :] * in_ref[side, a, :] for a in at[h]))

    far(0, s0_ref, y_ref)
    terms_e[0:lines, :] = p_ref[...] * (gr_ref[...] + in_ref[0] * ends_ref[1]) + lag_ref[...]
    terms_e[lines:first, :] = gskip_ref[...]
    for ref, used in ((terms_e, first + TAPS * nb), (terms_l, 2 * TAPS * nb)):
        if used < ref.shape[0]:
            ref[used:, :] = jnp.zeros((ref.shape[0] - used, LANES), F32)
    hits_t = ot_ref[...]
    wide_lanes = 2 * LANES

    def emit(f, k, lanes, val, ref, base):
        val = val.astype(BF16)
        fg_ref[f, :, lanes] = val
        head_ref[f, :, lanes] = val[:SUB, :]
        sums = jnp.dot(hits_t, val, preferred_element_type=F32)
        n4 = n4_ref[:, lanes]
        taps = jnp.concatenate(
            [jnp.sum(sums[i * SUB : (i + 1) * SUB, :] * n4, axis=0, keepdims=True) for i in range(TAPS)], 0
        )
        for s in range(2):
            ref[pl.ds(base + k * 2 + s, TAPS, stride=nb), :] = taps[:, s * LANES : (s + 1) * LANES]

    def along(ref, k):
        return jnp.concatenate([ref[pl.ds(k * 2 + s, length, stride=pitch), :] for s in range(2)], 1)

    def query_outputs(k, carry):
        lanes = pl.ds(pl.multiple_of(k * wide_lanes, wide_lanes), wide_lanes)
        y = along(y_ref, k)
        hyena_ref[:, lanes] = (feat_ref[0, :, lanes].astype(F32) * y).astype(BF16)
        emit(0, k, lanes, ct_ref[:, lanes].astype(F32) * y, terms_e, first)
        return carry

    def scatter(whole, ref, got_ref, send, recv):
        whole[...] = ref[...].astype(BF16)
        rows = whole.shape[0] // n_seq
        started = []
        for o in range(1, n_seq):
            mine = pl.ds(pl.multiple_of(peer[o] * rows, rows), rows)
            copy = remote(whole.at[mine, :], got_ref.at[o], send.at[o], recv.at[o], {"seq": peer[o]})
            copy.start()
            started.append(copy)
        return started

    def gather(started, whole, got_ref, total, sums, send, recv):
        rows = whole.shape[0] // n_seq
        mine = pl.ds(pl.multiple_of(me * rows, rows), rows)
        summed = whole[mine, :].astype(F32)
        for o in range(1, n_seq):
            started[o - 1].wait()
            summed = summed + got_ref[o].astype(F32)
        total[...] = summed.astype(BF16)
        started = []
        for o in range(1, n_seq):
            copy = remote(total, sums.at[mine, :], send.at[o], recv.at[o], {"seq": peer[o]})
            copy.start()
            started.append(copy)
        sums[mine, :] = summed.astype(BF16)
        return started

    lax.fori_loop(0, nb // 2, query_outputs, 0)
    e_copies = scatter(whole_e, terms_e, tgot_e, t_send, t_recv)
    for copy in a_copies:
        copy.wait()
    far(1, b0_ref, gm_ref)
    e_copies = gather(e_copies, whole_e, tgot_e, total_e, sums_e, tb_send, tb_recv)

    def key_outputs(k, carry):
        lanes = pl.ds(pl.multiple_of(k * wide_lanes, wide_lanes), wide_lanes)
        gm = along(gm_ref, k)
        emit(1, k, lanes, gm * feat_ref[2, :, lanes].astype(F32), terms_l, 0)
        emit(2, k, lanes, gm * feat_ref[1, :, lanes].astype(F32), terms_l, TAPS * nb)
        return carry

    lax.fori_loop(0, nb // 2, key_outputs, 0)
    l_copies = scatter(whole_l, terms_l, tgot_l, l_send, l_recv)
    halo = remote(head_ref, tail, halo_sem.at[2], halo_sem.at[3], {"seq": peer[n_seq - 1]})
    halo.start()
    keep = jnp.where(me < n_seq - 1, 1.0, 0.0).astype(F32)
    block = 64
    inner = length - block

    def filtered(k, begin, end, base):
        lanes = pl.ds(pl.multiple_of(k * LANES, LANES), LANES)
        w = [w_ref[f, i : i + 1, lanes] for f in range(3) for i in range(TAPS)]
        for b in range(begin, end, block):
            acc = jnp.zeros((block, LANES), F32)
            for f in range(3):
                for i in range(TAPS):
                    acc = acc + w[f * TAPS + i] * pad[f, b - base + i : b - base + i + block, :]
            gn_ref[b : b + block, lanes] = acc.astype(BF16)

    def inner_rows(k, carry):
        lanes = pl.ds(pl.multiple_of(k * LANES, LANES), LANES)
        for f in range(3):
            pad[f, 0:length, :] = fg_ref[f, :, lanes].astype(F32)
        filtered(k, 0, inner, 0)
        return carry

    def last_rows(k, carry):
        lanes = pl.ds(pl.multiple_of(k * LANES, LANES), LANES)
        for f in range(3):
            pad[f, 0:block, :] = fg_ref[f, inner:length, lanes].astype(F32)
            pad[f, block : block + SUB, :] = tail[f, :, lanes].astype(F32) * keep
        filtered(k, inner, length, inner)
        return carry

    lax.fori_loop(0, nb // 2, inner_rows, 0)
    l_copies = gather(l_copies, whole_l, tgot_l, total_l, sums_l, lb_send, lb_recv)
    lax.fori_loop(nb // 2, nb, inner_rows, 0)
    for copy in e_copies:
        copy.wait()
    wide_e[...] = sums_e[...].astype(F32)
    for k in range(nb):
        lanes = slice(k * LANES, (k + 1) * LANES)
        gr_out_ref[:, lanes] = wide_e[pl.ds(k, poles, stride=nb), :]
        gskip_out_ref[:, lanes] = wide_e[lines + k : lines + k + 1, :]
        conv_ref[0, :, lanes] = wide_e[pl.ds(first + k, TAPS, stride=nb), :]
    halo.wait()
    lax.fori_loop(0, nb, last_rows, 0)
    for copy in l_copies:
        copy.wait()
    wide_l[...] = sums_l[...].astype(F32)
    for k in range(nb):
        lanes = slice(k * LANES, (k + 1) * LANES)
        for f in range(1, 3):
            conv_ref[f, :, lanes] = wide_l[pl.ds((f - 1) * TAPS * nb + k, TAPS, stride=nb), :]


def finish_kernel(hyena_in, gn_in, conv_in, gr_in, gskip_in, hyena_ref, gn_ref, conv_ref, gr_ref, gskip_ref, sem):
    pairs = (
        (hyena_in, hyena_ref), (gn_in, gn_ref), (conv_in, conv_ref), (gr_in, gr_ref), (gskip_in, gskip_ref),
    )
    copies = [pltpu.make_async_copy(src, dst, sem.at[i]) for i, (src, dst) in enumerate(pairs)]
    for copy in copies:
        copy.start()
    for copy in copies:
        copy.wait()


def solution(mesh):
    n_seq, n_ch = mesh.shape["seq"], mesh.shape["ch"]
    dma = pltpu.SemaphoreType.DMA
    vmem = pltpu.VMEM

    def per_device(token_ids, embedding, norm_gain, conv_weight, pole_rates, residues, skip_gain, cotangent):
        length, chans = cotangent.shape
        poles = pole_rates.shape[0]
        nb = chans // LANES
        lines = poles * nb
        rp = lines // n_seq

        def reduced(rows):
            each = -(-rows // (16 * n_seq)) * 16
            return [
                vmem((each * n_seq, LANES), F32), vmem((each * n_seq, LANES), BF16), vmem((n_seq, each, LANES), BF16),
                vmem((each, LANES), BF16), vmem((each * n_seq, LANES), BF16), vmem((each * n_seq, LANES), F32),
            ]

        tile = vmem((length * (nb + GAP), LANES), F32)
        line = vmem((lines, LANES), F32)
        kept = vmem((length // CHUNK * lines, LANES), F32)
        scratch = [
            vmem((1, length), jnp.int32), vmem((1, chans), F32), vmem((3, TAPS, chans), F32),
            vmem((poles, chans), F32), vmem((poles, chans), F32), vmem((1, chans), F32), vmem((length, chans), BF16),
            dma((7,)),
            vmem((SUB, LANES), F32), vmem((n_ch, SUB, LANES), F32), vmem((1, length), jnp.int32),
            vmem((3, length, chans), BF16), tile, tile, vmem((8 * SUB, length), BF16), vmem((SUB, chans), F32),
            vmem((2, lines, LANES), F32), vmem((2, lines, LANES), F32), line, vmem((nb, LANES), F32),
            line, line, line, vmem((CHUNK * nb, LANES), F32), line, kept, kept, line, tile, tile, vmem((3, 16 * SUB, chans), BF16),
            vmem((2, n_seq, rp, LANES), F32), vmem((2, n_seq, rp, LANES), F32),
            vmem((3, length, chans), BF16), vmem((3, SUB, chans), BF16), vmem((3, SUB, chans), BF16),
            *reduced(lines + nb + TAPS * nb), *reduced(2 * TAPS * nb), vmem((3, length + SUB, LANES), F32),
            vmem((BAND, chans), BF16), dma, dma((n_ch,)), dma((n_ch,)), dma((4,)),
        ] + [dma((n_seq,))] * 16
        outs = [
            ((length, chans), BF16), ((length, chans), BF16), ((3, TAPS, chans), F32), ((poles, chans), F32),
            ((1, chans), F32),
        ]
        ins = (
            token_ids.reshape(1, length), embedding, norm_gain.reshape(1, chans), conv_weight, pole_rates, residues,
            skip_gain.reshape(1, chans), cotangent,
        )
        held = pl.pallas_call(
            functools.partial(mega_kernel, n_seq, n_ch, poles),
            out_shape=[pltpu.VMEM(shape, dtype) for shape, dtype in outs],
            in_specs=[
                pl.BlockSpec(memory_space=pl.ANY) for i in range(len(ins))
            ],
            out_specs=[pl.BlockSpec(memory_space=pltpu.VMEM)] * len(outs),
            scratch_shapes=scratch,
            compiler_params=pltpu.CompilerParams(
                vmem_limit_bytes=VLIMIT, collective_id=0, has_side_effects=True
            ),
        )(*ins)
        hyena, grad_normed, conv, gr, gskip = pl.pallas_call(
            finish_kernel,
            out_shape=[jax.ShapeDtypeStruct(shape, dtype) for shape, dtype in outs],
            in_specs=[pl.BlockSpec(memory_space=pltpu.VMEM)] * len(outs),
            out_specs=[pl.BlockSpec(memory_space=pl.ANY)] * len(outs),
            scratch_shapes=[dma((len(outs),))],
        )(*(pltpu.with_memory_space_constraint(part, pltpu.VMEM) for part in held))
        return hyena, grad_normed, conv, gr, gskip.reshape(chans)

    in_specs = (
        P("seq"), P(None, "ch"), P("ch"), P(None, None, "ch"), P(None, "ch"), P(None, "ch"), P("ch"), P("seq", "ch"),
    )
    out_specs = (P("seq", "ch"), P("seq", "ch"), P(None, None, "ch"), P(None, "ch"), P("ch"))
    return jax.shard_map(per_device, mesh=mesh, in_specs=in_specs, out_specs=out_specs, check_vma=False)
```

time: 52.6 us -> 42.9 us (0.82)
  Pallas kernels: 51.8 us -> 42.1 us
    pallas_call x1, Pallas kernels: 50.3 us -> 40.6 us  [per_device(): pl.pallas_call(functools.partial(mega_kernel, n_seq, n_ch, poles), out_sh...]
where the time goes in v2:
time: 42.9 us; the launch traced here: 42.7 us
  Pallas kernels  42.1 us (98%)
  between operations  0.64 us (1%)
    pallas_call x1, Pallas kernels, per_device(): pl.pallas_call(functools.partial(mega_kernel, n_seq, n_ch, poles), out_sh...  40.6 us
    pallas_call x1, Pallas kernels, per_device(): pl.pallas_call(finish_kernel, out_shape=[jax.ShapeDtypeStruct(shape, dtyp...  1.46 us

profile of v2, /device:TPU:0, one launch (start us, length us, event | category | flops | bytes accessed | tf_op | source)
XLA Modules:
  0.0 42.7 jit_solution(13047039610963725522)
XLA Ops:
  0.6 40.6 %shard_map.119 = (bf16[256,2048]{1,0:T(8,128)(2,1)S(1)}, bf16[256,2048]{1,0:T(8,128)(2,1)S(1)}, f32[3,7,2048]{2,1,0:T(8,128)S(1)}, f32[16,2048]{1,0:T(8,128)S(1)}, f32[1,2048]{1,0:T(1,128)S(1)}) custom-call(s32[1,256]{1,0:T(1,128)} %bitcast.6, bf16[512,2048]{1,0:T(8,128)(2,1)} %emb_ref.1, f32[1,2048]{1,0:T(1,128)} %bitcast.4, f32[3,7,2048]{2,1,0:T(8,128)} %w_in.1, ...), custom_call_target="tpu_custom_call" | custom-call | tf_op jit(solution)/shard_map/pallas_call | solution.py:480
  41.3 1.5 %shard_map.120 = (bf16[256,2048]{1,0:T(8,128)(2,1)}, bf16[256,2048]{1,0:T(8,128)(2,1)}, f32[3,7,2048]{2,1,0:T(8,128)}, f32[16,2048]{1,0:T(8,128)}, f32[1,2048]{1,0:T(1,128)}) custom-call(bf16[256,2048]{1,0:T(8,128)(2,1)S(1)} %get-tuple-element.15.hyena_in, bf16[256,2048]{1,0:T(8,128)(2,1)S(1)} %get-tuple-element.16.gn_in, ...), custom_call_target="tpu_custom_call" | custom-call | tf_op jit(solution)/shard_map/pallas_call | solution.py:492

commit v3 on v2

--- a/solution.py
+++ b/solution.py
@@ -46,7 +46,7 @@
     part, ss_got, prev_got, feat_ref, y_ref, gm_ref, ot_ref, n4_ref, ends_ref, in_ref, gr_ref, gskip_ref,
     p_ref, rp_ref, pc_ref, hs_ref, lag_ref, s0_ref, b0_ref, decay_ref, xs, gs, table, got, out, fg_ref, head_ref, tail,
     terms_e, whole_e, tgot_e, total_e, sums_e, wide_e, terms_l, whole_l, tgot_l, total_l, sums_l, wide_l, pad,
-    emb_rows, emb_sem, ss_send, ss_recv, halo_sem, f_send, f_recv, fb_send, fb_recv, a_send, a_recv, ab_send, ab_recv,
+    emb_rows, emb_sem, ss_send, ss_recv, halo_sem, x_send, x_recv, xb_send, xb_recv,
     t_send, t_recv, tb_send, tb_recv, l_send, l_recv, lb_send, lb_recv,
 ):
     me = lax.axis_index("seq")
@@ -79,7 +79,7 @@
     for k in range(nb):
         lanes = slice(k * LANES, (k + 1) * LANES)
         rates = rate_ref[:, lanes]
-        rows = pl.ds(k, poles, stride=nb)
+        rows = pl.ds(k // SUB * poles * SUB + k % SUB, poles, stride=SUB)
         p_ref[rows, :] = jnp.exp(-rates)
         decay_ref[rows, :] = jnp.exp(-rates * length)
         pc_ref[rows, :] = jnp.exp(-rates * CHUNK)
@@ -136,7 +136,7 @@
         table[f, 0 : 8 * SUB, :] = high
         table[f, 8 * SUB : 16 * SUB, :] = rest.astype(BF16)
 
-    def features(kb, carry):
+    def feature_block(kb):
         lanes = pl.ds(pl.multiple_of(kb * 256, 256), 256)
         parts = []
         for f in range(3):
@@ -148,49 +148,61 @@
         for s in range(2):
             xs[pl.ds(kb * 2 + s, length, stride=pitch), :] = x[:, s * LANES : (s + 1) * LANES]
             gs[pl.ds(kb * 2 + s, length, stride=pitch), :] = g[:, s * LANES : (s + 1) * LANES]
+
+    def features(step, carry):
+        for b in range(2):
+            feature_block(step * 2 + b)
         return carry
 
     loads[6].wait()
-    lax.fori_loop(0, chans // 256, features, 0)
-
-
-    rp = lines // n_seq
-    chunk = lambda k: pl.ds(pl.multiple_of(k * rp, rp), rp)
-
-    def send_ends(side, send, recv):
+    lax.fori_loop(0, chans // 512, features, 0)
+
+
+    own = min(n_seq, poles)
+    held = poles * SUB
+    rp = held // own
+    base = me // own * own
+    back = [base + lax.rem(me - base + o, own) for o in range(own)]
+
+    def chunk(k, h):
+        return pl.ds(pl.multiple_of(h * held + lax.rem(k, own) * rp, rp), rp)
+
+    def send_ends(side, h):
         started = []
         for o in range(1, n_seq):
             copy = remote(
-                ends_ref.at[side, chunk(peer[o]), :], got.at[side, me], send.at[o], recv.at[o], {"seq": peer[o]}
+                ends_ref.at[side, chunk(peer[o], h), :], got.at[side, h, me],
+                x_send.at[side, h, o], x_recv.at[side, h, o], {"seq": peer[o]},
             )
             copy.start()
             started.append(copy)
-        got[side, me] = ends_ref[side, chunk(me), :]
+        got[side, h, me] = ends_ref[side, chunk(me, h), :]
         return started
 
-    def send_carries(side, started, send, recv):
+    def send_carries(side, h, started):
         for copy in started:
             copy.wait()
-        decay = decay_ref[chunk(me), :]
+        decay = decay_ref[chunk(me, h), :]
         state = jnp.zeros_like(decay)
         for e in reversed(range(n_seq)) if side else range(n_seq):
-            out[side, e] = state
-            state = decay * state + got[side, e]
+            out[side, h, e] = state
+            state = decay * state + got[side, h, e]
         started = []
-        for o in range(1, n_seq):
+        for o in range(1, own):
             copy = remote(
-                out.at[side, peer[o]], in_ref.at[side, chunk(me), :], send.at[o], recv.at[o], {"seq": peer[o]}
+                out.at[side, h, back[o]], in_ref.at[side, chunk(me, h), :],
+                xb_send.at[side, h, o], xb_recv.at[side, h, o], {"seq": back[o]},
             )
             copy.start()
             started.append(copy)
-        in_ref[side, chunk(me), :] = out[side, me]
+        in_ref[side, chunk(me, h), :] = out[side, h, me]
         return started
 
     group = poles // 2
     zero = jnp.zeros((SUB, LANES), F32)
     halves = range(nb // SUB)
     chunks = length // CHUNK
-    at = [[pl.ds(n * nb + h * SUB, SUB) for n in range(poles)] for h in halves]
+    at = [[pl.ds((h * poles + n) * SUB, SUB) for n in range(poles)] for h in halves]
 
     def row(ref_row, h):
         return pl.ds(pl.multiple_of(ref_row * nb + h * SUB, SUB), SUB)
@@ -206,6 +218,7 @@
             ]
         return values[0]
 
+    f_copies = []
     for h in halves:
         for half in range(2):
             poles_of = range(half * group, (half + 1) * group)
@@ -227,8 +240,9 @@
             s = lax.fori_loop(0, chunks // PAIR, states, (zero,) * group)
             for i, n in enumerate(poles_of):
                 ends_ref[0, at[h][n], :] = s[i]
-
-    f_copies = send_ends(0, f_send, f_recv)
+        f_copies.append(send_ends(0, h))
+
+    a_copies = []
     for h in halves:
         for half in range(2):
             poles_of = range(half * group, (half + 1) * group)
@@ -252,8 +266,8 @@
             for i, n in enumerate(poles_of):
                 ends_ref[1, at[h][n], :] = s[i]
                 gr_ref[at[h][n], :] = acc[i]
-    f_copies = send_carries(0, f_copies, fb_send, fb_recv)
-    a_copies = send_ends(1, a_send, a_recv)
+        f_copies[h] = send_carries(0, h, f_copies[h])
+        a_copies.append(send_ends(1, h))
 
     for h in halves:
         taps = [hs_ref[row(d, h), :] for d in range(CHUNK)]
@@ -277,26 +291,26 @@
             for d in reversed(range(CHUNK - 1)):
                 total_lag = p * total_lag + lag[d]
             lag_ref[at[h][n], :] = total_lag
-    for copy in f_copies:
-        copy.wait()
-    a_copies = send_carries(1, a_copies, ab_send, ab_recv)
-
-    def far(side, kept, ref):
-        for h in halves:
-            p = [p_ref[at[h][n], :] for n in range(poles)]
-
-            def readout(step, w):
-                u = chunks - 1 - step if side else step
-                part = [rp_ref[at[h][n], :] * kept[row(u * poles + n, h), :] + w[n] for n in range(poles)]
-                for v in reversed(range(CHUNK)) if side else range(CHUNK):
-                    rows = time(u * CHUNK + v, h)
-                    ref[rows, :] = ref[rows, :] + tree(part)
-                    part = [part[n] * p[n] for n in range(poles)]
-                return tuple(w[n] * pc_ref[at[h][n], :] for n in range(poles))
-
-            lax.fori_loop(0, chunks, readout, tuple(rp_ref[a, :] * in_ref[side, a, :] for a in at[h]))
-
-    far(0, s0_ref, y_ref)
+
+    def far(side, h, started, kept, ref):
+        for copy in started:
+            copy.wait()
+        p = [p_ref[at[h][n], :] for n in range(poles)]
+
+        def readout(step, w):
+            u = chunks - 1 - step if side else step
+            part = [rp_ref[at[h][n], :] * kept[row(u * poles + n, h), :] + w[n] for n in range(poles)]
+            for v in reversed(range(CHUNK)) if side else range(CHUNK):
+                rows = time(u * CHUNK + v, h)
+                ref[rows, :] = ref[rows, :] + tree(part)
+                part = [part[n] * p[n] for n in range(poles)]
+            return tuple(w[n] * pc_ref[at[h][n], :] for n in range(poles))
+
+        lax.fori_loop(0, chunks, readout, tuple(rp_ref[a, :] * in_ref[side, a, :] for a in at[h]))
+
+    for h in halves:
+        a_copies[h] = send_carries(1, h, a_copies[h])
+        far(0, h, f_copies[h], s0_ref, y_ref)
     terms_e[0:lines, :] = p_ref[...] * (gr_ref[...] + in_ref[0] * ends_ref[1]) + lag_ref[...]
     terms_e[lines:first, :] = gskip_ref[...]
     for ref, used in ((terms_e, first + TAPS * nb), (terms_l, 2 * TAPS * nb)):
@@ -320,11 +334,14 @@
     def along(ref, k):
         return jnp.concatenate([ref[pl.ds(k * 2 + s, length, stride=pitch), :] for s in range(2)], 1)
 
-    def query_outputs(k, carry):
+    def query_outputs_block(k):
         lanes = pl.ds(pl.multiple_of(k * wide_lanes, wide_lanes), wide_lanes)
         y = along(y_ref, k)
-        hyena_ref[:, lanes] = (feat_ref[0, :, lanes].astype(F32) * y).astype(BF16)
         emit(0, k, lanes, ct_ref[:, lanes].astype(F32) * y, terms_e, first)
+
+    def query_outputs(step, carry):
+        for b in range(2):
+            query_outputs_block(step * 2 + b)
         return carry
 
     def scatter(whole, ref, got_ref, send, recv):
@@ -354,21 +371,25 @@
         sums[mine, :] = summed.astype(BF16)
         return started
 
-    lax.fori_loop(0, nb // 2, query_outputs, 0)
+    lax.fori_loop(0, nb // 4, query_outputs, 0)
     e_copies = scatter(whole_e, terms_e, tgot_e, t_send, t_recv)
-    for copy in a_copies:
-        copy.wait()
-    far(1, b0_ref, gm_ref)
-    e_copies = gather(e_copies, whole_e, tgot_e, total_e, sums_e, tb_send, tb_recv)
-
-    def key_outputs(k, carry):
+    for h in halves:
+        far(1, h, a_copies[h], b0_ref, gm_ref)
+        if h == 0:
+            e_copies = gather(e_copies, whole_e, tgot_e, total_e, sums_e, tb_send, tb_recv)
+
+    def key_outputs_block(k):
         lanes = pl.ds(pl.multiple_of(k * wide_lanes, wide_lanes), wide_lanes)
         gm = along(gm_ref, k)
         emit(1, k, lanes, gm * feat_ref[2, :, lanes].astype(F32), terms_l, 0)
         emit(2, k, lanes, gm * feat_ref[1, :, lanes].astype(F32), terms_l, TAPS * nb)
+
+    def key_outputs(step, carry):
+        for b in range(2):
+            key_outputs_block(step * 2 + b)
         return carry
 
-    lax.fori_loop(0, nb // 2, key_outputs, 0)
+    lax.fori_loop(0, nb // 4, key_outputs, 0)
     l_copies = scatter(whole_l, terms_l, tgot_l, l_send, l_recv)
     halo = remote(head_ref, tail, halo_sem.at[2], halo_sem.at[3], {"seq": peer[n_seq - 1]})
     halo.start()
@@ -401,15 +422,21 @@
         filtered(k, inner, length, inner)
         return carry
 
-    lax.fori_loop(0, nb // 2, inner_rows, 0)
+    def hyena_rows(k, carry):
+        lanes = pl.ds(pl.multiple_of(k * wide_lanes, wide_lanes), wide_lanes)
+        hyena_ref[:, lanes] = (feat_ref[0, :, lanes].astype(F32) * along(y_ref, k)).astype(BF16)
+        return carry
+
+    lax.fori_loop(0, nb // 2, hyena_rows, 0)
+    lax.fori_loop(0, 3 * nb // 4, inner_rows, 0)
     l_copies = gather(l_copies, whole_l, tgot_l, total_l, sums_l, lb_send, lb_recv)
-    lax.fori_loop(nb // 2, nb, inner_rows, 0)
+    lax.fori_loop(3 * nb // 4, nb, inner_rows, 0)
     for copy in e_copies:
         copy.wait()
     wide_e[...] = sums_e[...].astype(F32)
     for k in range(nb):
         lanes = slice(k * LANES, (k + 1) * LANES)
-        gr_out_ref[:, lanes] = wide_e[pl.ds(k, poles, stride=nb), :]
+        gr_out_ref[:, lanes] = wide_e[pl.ds(k // SUB * poles * SUB + k % SUB, poles, stride=SUB), :]
         gskip_out_ref[:, lanes] = wide_e[lines + k : lines + k + 1, :]
         conv_ref[0, :, lanes] = wide_e[pl.ds(first + k, TAPS, stride=nb), :]
     halo.wait()
@@ -444,7 +471,7 @@
         poles = pole_rates.shape[0]
         nb = chans // LANES
         lines = poles * nb
-        rp = lines // n_seq
+        rp = poles * SUB // min(n_seq, poles)
 
         def reduced(rows):
             each = -(-rows // (16 * n_seq)) * 16
@@ -464,11 +491,11 @@
             vmem((3, length, chans), BF16), tile, tile, vmem((8 * SUB, length), BF16), vmem((SUB, chans), F32),
             vmem((2, lines, LANES), F32), vmem((2, lines, LANES), F32), line, vmem((nb, LANES), F32),
             line, line, line, vmem((CHUNK * nb, LANES), F32), line, kept, kept, line, tile, tile, vmem((3, 16 * SUB, chans), BF16),
-            vmem((2, n_seq, rp, LANES), F32), vmem((2, n_seq, rp, LANES), F32),
+            vmem((2, nb // SUB, n_seq, rp, LANES), F32), vmem((2, nb // SUB, n_seq, rp, LANES), F32),
             vmem((3, length, chans), BF16), vmem((3, SUB, chans), BF16), vmem((3, SUB, chans), BF16),
             *reduced(lines + nb + TAPS * nb), *reduced(2 * TAPS * nb), vmem((3, length + SUB, LANES), F32),
             vmem((BAND, chans), BF16), dma, dma((n_ch,)), dma((n_ch,)), dma((4,)),
-        ] + [dma((n_seq,))] * 16
+        ] + [dma((2, nb // SUB, n_seq))] * 4 + [dma((n_seq,))] * 8
         outs = [
             ((length, chans), BF16), ((length, chans), BF16), ((3, TAPS, chans), F32), ((poles, chans), F32),
             ((1, chans), F32),

time: 42.9 us -> 41.2 us (0.960)
  Pallas kernels: 42.1 us -> 40.4 us
    pallas_call x1, Pallas kernels: 40.6 us -> 39 us  [per_device(): pl.pallas_call(functools.partial(mega_kernel, n_seq, n_ch, poles), out_sh...]
where the time goes in v3:
time: 41.2 us; the launch traced here: 41.1 us
  Pallas kernels  40.4 us (98%)
  between operations  0.64 us (2%)
    pallas_call x1, Pallas kernels, per_device(): pl.pallas_call(functools.partial(mega_kernel, n_seq, n_ch, poles), out_sh...  39 us
    pallas_call x1, Pallas kernels, per_device(): pl.pallas_call(finish_kernel, out_shape=[jax.ShapeDtypeStruct(shape, dtyp...  1.46 us

profile of v3, /device:TPU:0, one launch (start us, length us, event | category | flops | bytes accessed | tf_op | source)
XLA Modules:
  0.0 41.1 jit_solution(3378107857429162286)
XLA Ops:
  0.6 39.0 %shard_map.119 = (bf16[256,2048]{1,0:T(8,128)(2,1)S(1)}, bf16[256,2048]{1,0:T(8,128)(2,1)S(1)}, f32[3,7,2048]{2,1,0:T(8,128)S(1)}, f32[16,2048]{1,0:T(8,128)S(1)}, f32[1,2048]{1,0:T(1,128)S(1)}) custom-call(s32[1,256]{1,0:T(1,128)} %bitcast.6, bf16[512,2048]{1,0:T(8,128)(2,1)} %emb_ref.1, f32[1,2048]{1,0:T(1,128)} %bitcast.4, f32[3,7,2048]{2,1,0:T(8,128)} %w_in.1, ...), custom_call_target="tpu_custom_call" | custom-call | tf_op jit(solution)/shard_map/pallas_call | solution.py:507
  39.6 1.5 %shard_map.120 = (bf16[256,2048]{1,0:T(8,128)(2,1)}, bf16[256,2048]{1,0:T(8,128)(2,1)}, f32[3,7,2048]{2,1,0:T(8,128)}, f32[16,2048]{1,0:T(8,128)}, f32[1,2048]{1,0:T(1,128)}) custom-call(bf16[256,2048]{1,0:T(8,128)(2,1)S(1)} %get-tuple-element.15.hyena_in, bf16[256,2048]{1,0:T(8,128)(2,1)S(1)} %get-tuple-element.16.gn_in, ...), custom_call_target="tpu_custom_call" | custom-call | tf_op jit(solution)/shard_map/pallas_call | solution.py:519

commit v4 on v3

--- a/solution.py
+++ b/solution.py
@@ -91,8 +91,7 @@
             weight = weight * jnp.exp(-rates)
     fetch.wait()
     emb = jnp.concatenate(
-        [emb_rows[v - low_row : v - low_row + 1, :].astype(F32) for v in CODES]
-        + [jnp.zeros((SUB - len(CODES), chans), F32)],
+        [emb_rows[v - low_row : v - low_row + 1, :].astype(F32) for v in CODES] * 2,
         0,
     )
     squares = jnp.broadcast_to(jnp.sum(emb * emb, axis=1, keepdims=True), (SUB, LANES))
@@ -112,11 +111,13 @@
     row = lax.broadcasted_iota(jnp.int32, (SUB, length), 0)
     code = jnp.full((SUB, length), -2, jnp.int32)
     for a, value in enumerate(CODES):
-        code = jnp.where(row == a, value, code)
+        code = jnp.where(lax.rem(row, len(CODES)) == a, value, code)
     ext = jnp.concatenate([prev, ids_ref[...]], 1)
+    shifted = [ext[:, length - i : 2 * length - i] for i in range(TAPS)] + [jnp.full((1, length), -1, jnp.int32)]
     hits = [
-        jnp.where(ext[:, length - i : 2 * length - i] == code, 1.0, 0.0).astype(F32) for i in range(TAPS)
-    ] + [jnp.zeros((SUB, length), F32)]
+        jnp.where(jnp.where(row >= len(CODES), shifted[2 * j + 1], shifted[2 * j]) == code, 1.0, 0.0).astype(F32)
+        for j in range(SUB // 2)
+    ]
     onehot = jnp.concatenate(hits, 0)
     ot_ref[...] = onehot.astype(BF16)
     picks = jnp.transpose(jnp.concatenate([onehot] * 2, 0)).astype(BF16)
@@ -126,15 +127,14 @@
     scale = lax.rsqrt(squares / width + 1e-05)[:, :1]
     n4 = (emb * scale * gain_ref[...]).astype(BF16).astype(F32)
     n4_ref[...] = n4
-    zero_rows = jnp.zeros((SUB, chans), F32)
+    later = lax.broadcasted_iota(jnp.int32, (SUB, chans), 0) >= len(CODES)
     for f in range(3):
-        full = jnp.concatenate(
-            [w_ref[f, i : i + 1, :] * n4 for i in range(TAPS)] + [zero_rows], 0
-        )
+        w = [w_ref[f, i : i + 1, :] for i in range(TAPS)] + [jnp.zeros((1, chans), F32)]
+        full = jnp.concatenate([jnp.where(later, w[2 * j + 1], w[2 * j]) * n4 for j in range(SUB // 2)], 0)
         high = full.astype(BF16)
         rest = full - high.astype(F32)
-        table[f, 0 : 8 * SUB, :] = high
-        table[f, 8 * SUB : 16 * SUB, :] = rest.astype(BF16)
+        table[f, 0 : 4 * SUB, :] = high
+        table[f, 4 * SUB : 8 * SUB, :] = rest.astype(BF16)
 
     def feature_block(kb):
         lanes = pl.ds(pl.multiple_of(kb * 256, 256), 256)
@@ -272,7 +272,7 @@
     for h in halves:
         taps = [hs_ref[row(d, h), :] for d in range(CHUNK)]
 
-        def near(u, lag):
+        def near_chunk(u, lag):
             lag = list(lag)
             x = [xs[time(u * CHUNK + v, h), :] for v in range(CHUNK)]
             g = [gs[time(u * CHUNK + v, h), :] for v in range(CHUNK)]
@@ -283,7 +283,12 @@
                 lag[d] = lag[d] + tree(g[v + d] * x[v] for v in range(CHUNK - d))
             return tuple(lag)
 
-        lag = lax.fori_loop(0, chunks, near, (zero,) * CHUNK)
+        def near(step, lag):
+            for c in range(PAIR):
+                lag = near_chunk(step * PAIR + c, lag)
+            return lag
+
+        lag = lax.fori_loop(0, chunks // PAIR, near, (zero,) * CHUNK)
         gskip_ref[h * SUB : (h + 1) * SUB, :] = lag[0]
         for n in range(poles):
             p = p_ref[at[h][n], :]
@@ -297,7 +302,7 @@
             copy.wait()
         p = [p_ref[at[h][n], :] for n in range(poles)]
 
-        def readout(step, w):
+        def readout_chunk(step, w):
             u = chunks - 1 - step if side else step
             part = [rp_ref[at[h][n], :] * kept[row(u * poles + n, h), :] + w[n] for n in range(poles)]
             for v in reversed(range(CHUNK)) if side else range(CHUNK):
@@ -306,7 +311,12 @@
                 part = [part[n] * p[n] for n in range(poles)]
             return tuple(w[n] * pc_ref[at[h][n], :] for n in range(poles))
 
-        lax.fori_loop(0, chunks, readout, tuple(rp_ref[a, :] * in_ref[side, a, :] for a in at[h]))
+        def readout(step, w):
+            for c in range(PAIR):
+                w = readout_chunk(step * PAIR + c, w)
+            return w
+
+        lax.fori_loop(0, chunks // PAIR, readout, tuple(rp_ref[a, :] * in_ref[side, a, :] for a in at[h]))
 
     for h in halves:
         a_copies[h] = send_carries(1, h, a_copies[h])
@@ -325,9 +335,13 @@
         head_ref[f, :, lanes] = val[:SUB, :]
         sums = jnp.dot(hits_t, val, preferred_element_type=F32)
         n4 = n4_ref[:, lanes]
-        taps = jnp.concatenate(
-            [jnp.sum(sums[i * SUB : (i + 1) * SUB, :] * n4, axis=0, keepdims=True) for i in range(TAPS)], 0
-        )
+        taps = []
+        for i in range(SUB // 2):
+            pair = sums[i * SUB : (i + 1) * SUB, :] * n4
+            pair = pair + pltpu.roll(pair, 2, 0)
+            pair = pair + pltpu.roll(pair, 1, 0)
+            taps += [pair[len(CODES) - 1 : len(CODES), :], pair[SUB - 1 : SUB, :]]
+        taps = jnp.concatenate(taps[:TAPS], 0)
         for s in range(2):
             ref[pl.ds(base + k * 2 + s, TAPS, stride=nb), :] = taps[:, s * LANES : (s + 1) * LANES]
 
@@ -488,9 +502,9 @@
             vmem((poles, chans), F32), vmem((poles, chans), F32), vmem((1, chans), F32), vmem((length, chans), BF16),
             dma((7,)),
             vmem((SUB, LANES), F32), vmem((n_ch, SUB, LANES), F32), vmem((1, length), jnp.int32),
-            vmem((3, length, chans), BF16), tile, tile, vmem((8 * SUB, length), BF16), vmem((SUB, chans), F32),
+            vmem((3, length, chans), BF16), tile, tile, vmem((4 * SUB, length), BF16), vmem((SUB, chans), F32),
             vmem((2, lines, LANES), F32), vmem((2, lines, LANES), F32), line, vmem((nb, LANES), F32),
-            line, line, line, vmem((CHUNK * nb, LANES), F32), line, kept, kept, line, tile, tile, vmem((3, 16 * SUB, chans), BF16),
+            line, line, line, vmem((CHUNK * nb, LANES), F32), line, kept, kept, line, tile, tile, vmem((3, 8 * SUB, chans), BF16),
             vmem((2, nb // SUB, n_seq, rp, LANES), F32), vmem((2, nb // SUB, n_seq, rp, LANES), F32),
             vmem((3, length, chans), BF16), vmem((3, SUB, chans), BF16), vmem((3, SUB, chans), BF16),
             *reduced(lines + nb + TAPS * nb), *reduced(2 * TAPS * nb), vmem((3, length + SUB, LANES), F32),

time: 41.2 us -> 40.3 us (0.978)
  Pallas kernels: 40.4 us -> 39.5 us
    pallas_call x1, Pallas kernels: 39 us -> 38 us  [per_device(): pl.pallas_call(functools.partial(mega_kernel, n_seq, n_ch, poles), out_sh...]
where the time goes in v4:
time: 40.3 us; the launch traced here: 40.1 us
  Pallas kernels  39.5 us (98%)
  between operations  0.64 us (2%)
    pallas_call x1, Pallas kernels, per_device(): pl.pallas_call(functools.partial(mega_kernel, n_seq, n_ch, poles), out_sh...  38 us
    pallas_call x1, Pallas kernels, per_device(): pl.pallas_call(finish_kernel, out_shape=[jax.ShapeDtypeStruct(shape, dtyp...  1.46 us

profile of v4, /device:TPU:0, one launch (start us, length us, event | category | flops | bytes accessed | tf_op | source)
XLA Modules:
  0.0 40.1 jit_solution(8743042672971782163)
XLA Ops:
  0.6 38.0 %shard_map.119 = (bf16[256,2048]{1,0:T(8,128)(2,1)S(1)}, bf16[256,2048]{1,0:T(8,128)(2,1)S(1)}, f32[3,7,2048]{2,1,0:T(8,128)S(1)}, f32[16,2048]{1,0:T(8,128)S(1)}, f32[1,2048]{1,0:T(1,128)S(1)}) custom-call(s32[1,256]{1,0:T(1,128)} %bitcast.6, bf16[512,2048]{1,0:T(8,128)(2,1)} %emb_ref.1, f32[1,2048]{1,0:T(1,128)} %bitcast.4, f32[3,7,2048]{2,1,0:T(8,128)} %w_in.1, ...), custom_call_target="tpu_custom_call" | custom-call | tf_op jit(solution)/shard_map/pallas_call | solution.py:521
  38.7 1.5 %shard_map.120 = (bf16[256,2048]{1,0:T(8,128)(2,1)}, bf16[256,2048]{1,0:T(8,128)(2,1)}, f32[3,7,2048]{2,1,0:T(8,128)}, f32[16,2048]{1,0:T(8,128)}, f32[1,2048]{1,0:T(1,128)}) custom-call(bf16[256,2048]{1,0:T(8,128)(2,1)S(1)} %get-tuple-element.15.hyena_in, bf16[256,2048]{1,0:T(8,128)(2,1)S(1)} %get-tuple-element.16.gn_in, ...), custom_call_target="tpu_custom_call" | custom-call | tf_op jit(solution)/shard_map/pallas_call | solution.py:533

commit v5 on v4

--- a/solution.py
+++ b/solution.py
@@ -150,12 +150,12 @@
             gs[pl.ds(kb * 2 + s, length, stride=pitch), :] = g[:, s * LANES : (s + 1) * LANES]
 
     def features(step, carry):
-        for b in range(2):
-            feature_block(step * 2 + b)
+        for b in range(4):
+            feature_block(step * 4 + b)
         return carry
 
     loads[6].wait()
-    lax.fori_loop(0, chans // 512, features, 0)
+    lax.fori_loop(0, chans // 1024, features, 0)
 
 
     own = min(n_seq, poles)
@@ -354,8 +354,8 @@
         emit(0, k, lanes, ct_ref[:, lanes].astype(F32) * y, terms_e, first)
 
     def query_outputs(step, carry):
-        for b in range(2):
-            query_outputs_block(step * 2 + b)
+        for b in range(4):
+            query_outputs_block(step * 4 + b)
         return carry
 
     def scatter(whole, ref, got_ref, send, recv):
@@ -385,7 +385,7 @@
         sums[mine, :] = summed.astype(BF16)
         return started
 
-    lax.fori_loop(0, nb // 4, query_outputs, 0)
+    lax.fori_loop(0, nb // 8, query_outputs, 0)
     e_copies = scatter(whole_e, terms_e, tgot_e, t_send, t_recv)
     for h in halves:
         far(1, h, a_copies[h], b0_ref, gm_ref)
@@ -399,11 +399,11 @@
         emit(2, k, lanes, gm * feat_ref[1, :, lanes].astype(F32), terms_l, TAPS * nb)
 
     def key_outputs(step, carry):
-        for b in range(2):
-            key_outputs_block(step * 2 + b)
+        for b in range(4):
+            key_outputs_block(step * 4 + b)
         return carry
 
-    lax.fori_loop(0, nb // 4, key_outputs, 0)
+    lax.fori_loop(0, nb // 8, key_outputs, 0)
     l_copies = scatter(whole_l, terms_l, tgot_l, l_send, l_recv)
     halo = remote(head_ref, tail, halo_sem.at[2], halo_sem.at[3], {"seq": peer[n_seq - 1]})
     halo.start()

time: 40.3 us -> 39.5 us (0.980)
  Pallas kernels: 39.5 us -> 38.7 us
    pallas_call x1, Pallas kernels: 38 us -> 37.3 us  [per_device(): pl.pallas_call(functools.partial(mega_kernel, n_seq, n_ch, poles), out_sh...]
where the time goes in v5:
time: 39.5 us; the launch traced here: 39.4 us
  Pallas kernels  38.7 us (98%)
  between operations  0.64 us (2%)
    pallas_call x1, Pallas kernels, per_device(): pl.pallas_call(functools.partial(mega_kernel, n_seq, n_ch, poles), out_sh...  37.3 us
    pallas_call x1, Pallas kernels, per_device(): pl.pallas_call(finish_kernel, out_shape=[jax.ShapeDtypeStruct(shape, dtyp...  1.46 us

profile of v5, /device:TPU:0, one launch (start us, length us, event | category | flops | bytes accessed | tf_op | source)
XLA Modules:
  0.0 39.4 jit_solution(9272735512075044699)
XLA Ops:
  0.6 37.3 %shard_map.119 = (bf16[256,2048]{1,0:T(8,128)(2,1)S(1)}, bf16[256,2048]{1,0:T(8,128)(2,1)S(1)}, f32[3,7,2048]{2,1,0:T(8,128)S(1)}, f32[16,2048]{1,0:T(8,128)S(1)}, f32[1,2048]{1,0:T(1,128)S(1)}) custom-call(s32[1,256]{1,0:T(1,128)} %bitcast.6, bf16[512,2048]{1,0:T(8,128)(2,1)} %emb_ref.1, f32[1,2048]{1,0:T(1,128)} %bitcast.4, f32[3,7,2048]{2,1,0:T(8,128)} %w_in.1, ...), custom_call_target="tpu_custom_call" | custom-call | tf_op jit(solution)/shard_map/pallas_call | solution.py:521
  37.9 1.5 %shard_map.120 = (bf16[256,2048]{1,0:T(8,128)(2,1)}, bf16[256,2048]{1,0:T(8,128)(2,1)}, f32[3,7,2048]{2,1,0:T(8,128)}, f32[16,2048]{1,0:T(8,128)}, f32[1,2048]{1,0:T(1,128)}) custom-call(bf16[256,2048]{1,0:T(8,128)(2,1)S(1)} %get-tuple-element.15.hyena_in, bf16[256,2048]{1,0:T(8,128)(2,1)S(1)} %get-tuple-element.16.gn_in, ...), custom_call_target="tpu_custom_call" | custom-call | tf_op jit(solution)/shard_map/pallas_call | solution.py:533
